TPU v7x, 128 devices: a whole 4x4x4 slice. The times are simulated.
128 devices in a mesh: seq: 32 (over x, y, core), head: 4 (over z).
Axes of the slice: x: 4, y: 4, z: 4, core: 2. Of those that a mesh axis runs over, the one named last changes fastest.
Arguments:
- queries: bfloat16 [16384, 4096], P('seq', 'head'), may hold values from -7 to 7
- keys: bfloat16 [131072, 1024], P('seq', 'head'), may hold values from -4 to 4
- values: bfloat16 [131072, 1024], P('seq', 'head'), may hold values from -5 to 5
- out_grad: bfloat16 [16384, 4096], P('seq', 'head'), may hold values from -6 to 6
- out_weight: bfloat16 [4096, 4096], P('head'), may hold values from -0.09375 to 0.09375
- selected: int32 [32, 6], replicated, may hold values from 0 to 255, as said below
Outputs:
- query_grad: bfloat16 [16384, 4096], P('seq', 'head')
- key_grad: bfloat16 [131072, 1024], P('seq', 'head')
- value_grad: bfloat16 [131072, 1024], P('seq', 'head')
Inputs may be any that keep to these rules, and one draw needn't show every extreme that they name: `selected`: row i lists first the block i * 8 + 7, then 5 further distinct blocks of lower number; among them at most one lies in the run of 8 blocks j * 8 to j * 8 + 7 of any j other than i, and every row i >= 1 lists exactly one block of the run of j = 0.
All inputs are finite; a program needn't handle non-finite values.
Results may differ from a plain program's by a relative error of at most 0.0095.
Values may be sent and summed in bfloat16 or wider, within the bound.
A program may use at most 128 MiB of HBM per device.

v0:
```python
import jax
import jax.numpy as jnp
from jax import lax
from jax.sharding import PartitionSpec as P

HEAD_DIM = 128
BLOCK = 512
TOPK = 6


def in_one_piece(arrays, axis, split_dim, concat_dim, along):
    widths = [a.shape[along] for a in arrays]
    both = jnp.concatenate(arrays, axis=along)
    result = lax.all_to_all(both, axis, split_axis=split_dim, concat_axis=concat_dim, tiled=True)
    return tuple(jnp.split(result, [sum(widths[:k]) for k in range(1, len(widths))], axis=along))


def score_tile(query_head, key_head, factor, visible):
    scores = (
        lax.dot_general(
            query_head, key_head, (((1,), (1,)), ((), ())), preferred_element_type=jnp.float32
        )
        * factor
    )
    return jnp.where(visible, scores, -jnp.inf)


def shards(queries, keys, values, out_grad, out_weight, selected):
    factor = HEAD_DIM ** (-0.5)
    kv_cols = keys.shape[1]
    kv_local = kv_cols // HEAD_DIM
    q_local = queries.shape[1] // HEAD_DIM
    group_size = q_local // kv_local
    blocks_here = keys.shape[0] // BLOCK
    length = TOPK * BLOCK
    devices = lax.axis_size("seq")
    piece_rows = BLOCK // devices
    grad_output = lax.dot_general(
        lax.all_gather(out_grad, "head", axis=1, tiled=True),
        out_weight,
        (((1,), (1,)), ((), ())),
        preferred_element_type=jnp.float32,
    ).astype(jnp.bfloat16)
    key_tiles = keys.reshape(blocks_here, BLOCK, kv_cols)
    value_tiles = values.reshape(blocks_here, BLOCK, kv_cols)
    flat_pick = jnp.transpose(selected % blocks_here * devices + selected // blocks_here).reshape(
        -1
    )
    column = lax.broadcasted_iota(jnp.int32, (BLOCK, length), 1)
    rowpos = lax.broadcasted_iota(jnp.int32, (BLOCK, length), 0)
    visible = (column >= BLOCK) | (column <= rowpos)
    spread_keys, spread_values = in_one_piece(
        (
            key_tiles.reshape(blocks_here, devices, piece_rows, kv_cols),
            value_tiles.reshape(blocks_here, devices, piece_rows, kv_cols),
        ),
        "seq",
        1,
        1,
        0,
    )
    pool_keys = spread_keys.reshape(blocks_here * devices, piece_rows, kv_cols)
    pool_values = spread_values.reshape(blocks_here * devices, piece_rows, kv_cols)
    pick_keys = jnp.take(pool_keys, flat_pick, axis=0).reshape(TOPK, devices, piece_rows, kv_cols)
    pick_values = jnp.take(pool_values, flat_pick, axis=0).reshape(
        TOPK, devices, piece_rows, kv_cols
    )
    got_keys, got_values = in_one_piece((pick_keys, pick_values), "seq", 1, 1, 0)
    slot_keys = got_keys.reshape(length, kv_cols)
    slot_values = got_values.reshape(length, kv_cols)

    def one_head(head_index, running):
        query_acc, key_acc, value_acc = running
        kv_index = head_index // group_size
        query_head = lax.dynamic_slice_in_dim(queries, head_index * HEAD_DIM, HEAD_DIM, 1)
        grad_head = lax.dynamic_slice_in_dim(grad_output, head_index * HEAD_DIM, HEAD_DIM, 1)
        key_head = lax.dynamic_slice_in_dim(slot_keys, kv_index * HEAD_DIM, HEAD_DIM, 1)
        value_head = lax.dynamic_slice_in_dim(slot_values, kv_index * HEAD_DIM, HEAD_DIM, 1)
        scores = score_tile(query_head, key_head, factor, visible)
        row_max = jnp.max(scores, axis=1, keepdims=True)
        shifted = jnp.exp(scores - row_max)
        weights = shifted / jnp.sum(shifted, axis=1, keepdims=True)
        weights_low = weights.astype(jnp.bfloat16)
        attended = jnp.dot(weights_low, value_head, preferred_element_type=jnp.float32)
        row_dot = jnp.sum(grad_head.astype(jnp.float32) * attended, axis=1, keepdims=True)
        value_part = lax.dot_general(
            weights_low, grad_head, (((0,), (0,)), ((), ())), preferred_element_type=jnp.float32
        )
        grad_weights = lax.dot_general(
            grad_head, value_head, (((1,), (1,)), ((), ())), preferred_element_type=jnp.float32
        )
        grad_low = (weights * (grad_weights - row_dot)).astype(jnp.bfloat16)
        query_part = jnp.dot(grad_low, key_head, preferred_element_type=jnp.float32) * factor
        key_part = (
            lax.dot_general(
                grad_low, query_head, (((0,), (0,)), ((), ())), preferred_element_type=jnp.float32
            )
            * factor
        )
        query_acc = lax.dynamic_update_slice_in_dim(query_acc, query_part, head_index * HEAD_DIM, 1)
        old_key = lax.dynamic_slice_in_dim(key_acc, kv_index * HEAD_DIM, HEAD_DIM, 1)
        key_acc = lax.dynamic_update_slice_in_dim(
            key_acc, old_key + key_part, kv_index * HEAD_DIM, 1
        )
        old_value = lax.dynamic_slice_in_dim(value_acc, kv_index * HEAD_DIM, HEAD_DIM, 1)
        value_acc = lax.dynamic_update_slice_in_dim(
            value_acc, old_value + value_part, kv_index * HEAD_DIM, 1
        )
        return (query_acc, key_acc, value_acc)

    initial_acc = (
        jnp.zeros((BLOCK, q_local * HEAD_DIM), jnp.float32),
        jnp.zeros((length, kv_cols), jnp.float32),
        jnp.zeros((length, kv_cols), jnp.float32),
    )
    query_acc, key_acc, value_acc = lax.fori_loop(0, q_local, one_head, initial_acc)
    query_grad = query_acc.astype(jnp.bfloat16)
    key_low = key_acc.astype(jnp.bfloat16).reshape(TOPK, BLOCK, kv_cols)
    value_low = value_acc.astype(jnp.bfloat16).reshape(TOPK, BLOCK, kv_cols)
    came_keys, came_values = in_one_piece(
        (
            key_low.reshape(TOPK, devices, piece_rows, kv_cols),
            value_low.reshape(TOPK, devices, piece_rows, kv_cols),
        ),
        "seq",
        1,
        1,
        0,
    )
    pool_ids = jnp.arange(blocks_here * devices, dtype=jnp.int32)[:, None]
    collect = (flat_pick[None, :] == pool_ids).astype(jnp.bfloat16)
    key_pool = (
        jnp.dot(
            collect,
            came_keys.reshape(TOPK * devices, piece_rows * kv_cols),
            preferred_element_type=jnp.float32,
        )
        .astype(jnp.bfloat16)
        .reshape(blocks_here, devices, piece_rows, kv_cols)
    )
    value_pool = (
        jnp.dot(
            collect,
            came_values.reshape(TOPK * devices, piece_rows * kv_cols),
            preferred_element_type=jnp.float32,
        )
        .astype(jnp.bfloat16)
        .reshape(blocks_here, devices, piece_rows, kv_cols)
    )
    home_keys, home_values = in_one_piece((key_pool, value_pool), "seq", 1, 1, 0)
    key_grad = home_keys.reshape(blocks_here * BLOCK, kv_cols)
    value_grad = home_values.reshape(blocks_here * BLOCK, kv_cols)
    return (query_grad, key_grad, value_grad)


def solution(mesh):
    in_specs = (
        P("seq", "head"),
        P("seq", "head"),
        P("seq", "head"),
        P("seq", "head"),
        P("head", None),
        P(),
    )
    out_specs = (P("seq", "head"), P("seq", "head"), P("seq", "head"))
    return jax.shard_map(shards, mesh=mesh, in_specs=in_specs, out_specs=out_specs, check_vma=False)
```

profile of v0, /device:TPU:1, one launch (start us, length us, event | category | flops | bytes accessed | tf_op | source)
XLA Modules:
  0.0 437.9 jit_solution(4848488081770161708)
XLA Ops:
  12.3 8.8 %all-to-all-start = ((bf16[16,32,16,256]{3,2,0,1:T(8,128)(2,1)}), bf16[16,32,16,256]{3,2,0,1:T(8,128)(2,1)}, u32[]{:S(2)}, u32[]{:S(2)}) async-start(bf16[16,32,16,256]{3,2,0,1:T(8,128)(2,1)} %copy.13), calls=%async_computation | async-start | bytes 8388608 | tf_op jit(solution)/shard_map/all_to_all | solution.py:14
  21.9 51.3 %all-to-all-done = bf16[16,32,16,256]{3,2,0,1:T(8,128)(2,1)} async-done(((bf16[16,32,16,256]{3,2,0,1:T(8,128)(2,1)}), bf16[16,32,16,256]{3,2,0,1:T(8,128)(2,1)}, u32[]{:S(2)}, u32[]{:S(2)}) %all-to-all-start) | async-done | bytes 4194336 | tf_op jit(solution)/shard_map/all_to_all | solution.py:14
  85.2 7.1 %all-to-all-start.1 = ((bf16[12,32,16,256]{3,2,0,1:T(8,128)(2,1)}), bf16[12,32,16,256]{3,2,0,1:T(8,128)(2,1)S(1)}, u32[]{:S(2)}, u32[]{:S(2)}) async-start(bf16[12,32,16,256]{3,2,0,1:T(8,128)(2,1)} %copy.16), calls=%async_computation.1 | async-start | bytes 6291456 | tf_op jit(solution)/shard_map/all_to_all | solution.py:14
  92.4 10.1 %convolution_convert_fusion.2 = bf16[512,1024]{1,0:T(8,128)(2,1)} fusion(bf16[512,4096]{1,0:T(8,128)(2,1)} %all-gather.2.cloned.1.call-done, bf16[1024,4096]{1,0:T(8,128)(2,1)} %param.14), kind=kOutput, calls=%fused_computation.42 | convolution fusion | flops 4295491584 | bytes 13631488 | tf_op jit(solution)/shard_map/dot_general | solution.py:38
  102.5 29.6 %all-to-all-done.1 = bf16[12,32,16,256]{3,2,0,1:T(8,128)(2,1)S(1)} async-done(((bf16[12,32,16,256]{3,2,0,1:T(8,128)(2,1)}), bf16[12,32,16,256]{3,2,0,1:T(8,128)(2,1)S(1)}, u32[]{:S(2)}, u32[]{:S(2)}) %all-to-all-start.1) | async-done | bytes 3145760 | tf_op jit(solution)/shard_map/all_to_all | solution.py:14
  138.1 182.5 %while.20 = (s32[]{:T(128)}, bf16[512,1024]{1,0:T(8,128)(2,1)}, f32[3072,256]{1,0:T(8,128)S(1)}, f32[3072,256]{1,0:T(8,128)}, bf16[512,1024]{1,0:T(8,128)(2,1)},...) while((s32[]{:T(128)}, bf16[512,1024]{1,0:T(8,128)(2,1)}, ...), condition=%wide.region_4.6_spmd.clone, body=%wide.region_0.5_spmd.clone.sunk | while | flops 2439379456 | bytes 95831456 | solution.py:116
  141.4 3.9 fusion.80
  146.4 4.3 fusion.81
  157.2 3.7 fusion.84
  164.2 3.9 fusion.80
  169.2 4.3 fusion.81
  180.0 3.7 fusion.84
  187.1 3.9 fusion.80
  192.0 4.3 fusion.81
  202.9 3.7 fusion.84
  209.9 3.9 fusion.80
  214.9 4.3 fusion.81
  225.7 3.7 fusion.84
  232.7 3.9 fusion.80
  237.7 4.3 fusion.81
  248.5 3.6 fusion.84
  255.5 3.9 fusion.80
  260.5 4.3 fusion.81
  271.3 3.6 fusion.84
  278.3 3.9 fusion.80
  283.3 4.3 fusion.81
  294.1 3.6 fusion.84
  301.1 3.9 fusion.80
  306.1 4.3 fusion.81
  316.9 3.6 fusion.84
  323.4 44.2 %all_to_all.20 = bf16[12,32,16,256]{3,2,0,1:T(8,128)(2,1)S(1)} all-to-all(bf16[12,32,16,256]{3,2,0,1:T(8,128)(2,1)S(1)} %copy.20), channel_id=1, replica_groups=mesh['seq'=32,'head'=4] {'seq'}, dimensions={1} | all-to-all | bytes 6291456 | tf_op jit(solution)/shard_map/all_to_all | solution.py:14
  373.2 54.4 %all_to_all.21 = bf16[16,32,16,256]{3,2,0,1:T(8,128)(2,1)S(1)} all-to-all(bf16[16,32,16,256]{3,2,0,1:T(8,128)(2,1)S(1)} %copy.27), channel_id=1, replica_groups=mesh['seq'=32,'head'=4] {'seq'}, dimensions={1} | all-to-all | bytes 8388608 | tf_op jit(solution)/shard_map/all_to_all | solution.py:14
  (135 shorter events, 122.7 us)
Async XLA Ops:
  12.3 9.5 %copy-start.3 = (s32[32,6]{0,1:T(8,128)S(1)}, s32[32,6]{0,1:T(8,128)}, u32[]{:S(2)}) copy-start(s32[32,6]{0,1:T(8,128)} %param.15) | copy-start | bytes 2308
  12.3 61.0 %all-to-all-start = ((bf16[16,32,16,256]{3,2,0,1:T(8,128)(2,1)}), bf16[16,32,16,256]{3,2,0,1:T(8,128)(2,1)}, u32[]{:S(2)}, u32[]{:S(2)}) async-start(bf16[16,32,16,256]{3,2,0,1:T(8,128)(2,1)} %copy.13), calls=%async_computation | async-start | bytes 8388608 | tf_op jit(solution)/shard_map/all_to_all | solution.py:14
  21.1 71.3 %all-gather.2.cloned.1.call-start = ((), (), s32[]{:S(2)}) async-start(), calls=%async_computation.4 | async-start | bytes 5242880 | tf_op jit(solution)/shard_map/all_gather | solution.py:39
  79.5 2.6 copy-start.2
  85.2 46.9 %all-to-all-start.1 = ((bf16[12,32,16,256]{3,2,0,1:T(8,128)(2,1)}), bf16[12,32,16,256]{3,2,0,1:T(8,128)(2,1)S(1)}, u32[]{:S(2)}, u32[]{:S(2)}) async-start(bf16[12,32,16,256]{3,2,0,1:T(8,128)(2,1)} %copy.16), calls=%async_computation.1 | async-start | bytes 6291456 | tf_op jit(solution)/shard_map/all_to_all | solution.py:14
  146.4 4.8 %copy-start = (f32[512,3072]{1,0:T(8,128)S(1)}, f32[512,3072]{1,0:T(8,128)}, u32[]{:S(2)}) copy-start(f32[512,3072]{1,0:T(8,128)} %fusion.80) | copy-start | bytes 18874372 | tf_op jit(solution)/shard_map/while
  153.3 2.2 copy-start.1
  169.2 4.8 %copy-start = (f32[512,3072]{1,0:T(8,128)S(1)}, f32[512,3072]{1,0:T(8,128)}, u32[]{:S(2)}) copy-start(f32[512,3072]{1,0:T(8,128)} %fusion.80) | copy-start | bytes 18874372 | tf_op jit(solution)/shard_map/while
  176.2 2.2 copy-start.1
  192.0 4.8 %copy-start = (f32[512,3072]{1,0:T(8,128)S(1)}, f32[512,3072]{1,0:T(8,128)}, u32[]{:S(2)}) copy-start(f32[512,3072]{1,0:T(8,128)} %fusion.80) | copy-start | bytes 18874372 | tf_op jit(solution)/shard_map/while
  199.0 2.2 copy-start.1
  214.9 4.8 %copy-start = (f32[512,3072]{1,0:T(8,128)S(1)}, f32[512,3072]{1,0:T(8,128)}, u32[]{:S(2)}) copy-start(f32[512,3072]{1,0:T(8,128)} %fusion.80) | copy-start | bytes 18874372 | tf_op jit(solution)/shard_map/while
  221.8 2.2 copy-start.1
  237.7 4.8 %copy-start = (f32[512,3072]{1,0:T(8,128)S(1)}, f32[512,3072]{1,0:T(8,128)}, u32[]{:S(2)}) copy-start(f32[512,3072]{1,0:T(8,128)} %fusion.80) | copy-start | bytes 18874372 | tf_op jit(solution)/shard_map/while
  244.6 2.2 copy-start.1
  260.5 4.8 %copy-start = (f32[512,3072]{1,0:T(8,128)S(1)}, f32[512,3072]{1,0:T(8,128)}, u32[]{:S(2)}) copy-start(f32[512,3072]{1,0:T(8,128)} %fusion.80) | copy-start | bytes 18874372 | tf_op jit(solution)/shard_map/while
  267.4 2.2 copy-start.1
  283.3 4.8 %copy-start = (f32[512,3072]{1,0:T(8,128)S(1)}, f32[512,3072]{1,0:T(8,128)}, u32[]{:S(2)}) copy-start(f32[512,3072]{1,0:T(8,128)} %fusion.80) | copy-start | bytes 18874372 | tf_op jit(solution)/shard_map/while
  290.2 2.2 copy-start.1
  306.1 4.8 %copy-start = (f32[512,3072]{1,0:T(8,128)S(1)}, f32[512,3072]{1,0:T(8,128)}, u32[]{:S(2)}) copy-start(f32[512,3072]{1,0:T(8,128)} %fusion.80) | copy-start | bytes 18874372 | tf_op jit(solution)/shard_map/while
  313.0 2.2 copy-start.1
Sparse Core Ops, SparseCore 0:
  23.6 50.4 all-gather.1
where the time goes:
time: 439 us; the launch traced here: 438 us
  matrix products  142 us (32%)
  blocking collectives  98.5 us (22%)
  waiting for transfers between devices  81.6 us (19%)
  other arithmetic  46 us (10%)
  local copies, waits for them, and re-layouts  39.5 us (9%)
  starting transfers between devices  15.9 us (4%)
  between operations  14.2 us (3%)
    all_to_all x2, blocking collectives, in_one_piece(): lax.all_to_all(both, axis, split_axis=split_dim, concat_axis=concat_dim,...  98.5 us
    all_to_all x2, waiting for transfers between devices, in_one_piece(): lax.all_to_all(both, axis, split_axis=split_dim, concat_axis=concat_dim,...  80.9 us
    dot_general x8, matrix products, one_head(): jnp.dot(weights_low, value_head, preferred_element_type=jnp.float32)  34.3 us
    div x8, other arithmetic, one_head(): weights = shifted / jnp.sum(shifted, axis=1, keepdims=True)  31.5 us
    dot_general x8, matrix products, one_head(): lax.dot_general(weights_low, grad_head, (((0,), (0,)), ((), ())), preferr...  29.2 us
    dot_general x8, matrix products, score_tile(): lax.dot_general(query_head, key_head, (((1,), (1,)), ((), ())), preferred...  18.8 us
    dot_general x8, matrix products, one_head(): lax.dot_general(grad_low, query_head, (((0,), (0,)), ((), ())), preferred...  17.6 us
    dot_general x8, matrix products, one_head(): lax.dot_general(grad_head, value_head, (((1,), (1,)), ((), ())), preferre...  16.9 us
  transfers between devices with their start and end apart: 3, of which 2 were waited for; matrix products, arithmetic and copies ran while one was open for 5% of the time, Pallas kernels for 0%

commit v1 on v0

v1 whole, which is shorter than its diff:
```python
import functools
import math

import jax
import jax.numpy as jnp
from jax import lax
from jax.experimental import pallas as pl
from jax.experimental.pallas import tpu as pltpu
from jax.sharding import PartitionSpec as P

HEAD_DIM = 128
BLOCK = 512
TOPK = 6
SEQ = 32
ZDEV = 4
RUN = 8
PIECE = BLOCK // SEQ
SLOTS = TOPK - 1
KBLOCKS = SEQ * RUN
HEADS_HERE = 8
KV_HERE = 2
GROUP = HEADS_HERE // KV_HERE
FACTOR = HEAD_DIM**-0.5
EXP2_SCALE = FACTOR * math.log2(math.e)
MESH = pl.DeviceIdType.MESH

OFFSETS = [
    (1, 0), (3, 0), (0, 1), (0, 3), (1, 1), (3, 3), (1, 3), (3, 1),
    (2, 0), (0, 2), (1, 2), (3, 2), (2, 1), (2, 3), (2, 2),
]
DX_CODE = sum(dx * 4**t for t, (dx, _) in enumerate(OFFSETS))
DY_CODE = sum(dy * 4**t for t, (_, dy) in enumerate(OFFSETS))


def each_peer(me, visit):
    x, y, core = me // 8, me // 2 % 4, me % 2

    def step(flip, codes):
        dx_code, dy_code = codes
        peer = (x + dx_code % 4) % 4 * 8 + (y + dy_code % 4) % 4 * 2 + (core + flip) % 2
        visit(peer)
        return dx_code // 4, dy_code // 4

    for flip in (0, 1):
        lax.fori_loop(
            0,
            len(OFFSETS),
            lambda t, codes, flip=flip: step(flip, codes),
            (jnp.int32(DX_CODE), jnp.int32(DY_CODE)),
        )
    visit(x * 8 + y * 2 + 1 - core)


def dot_nt(a, b):
    return lax.dot_general(a, b, (((1,), (1,)), ((), ())), preferred_element_type=jnp.float32)


def dot_nn(a, b):
    return jnp.dot(a, b, preferred_element_type=jnp.float32)


def dot_tn(a, b):
    return lax.dot_general(a, b, (((0,), (0,)), ((), ())), preferred_element_type=jnp.float32)


def head_cols(index):
    return pl.ds(index * HEAD_DIM, HEAD_DIM)


def kernel(
    picks, table, q_hbm, k_hbm, v_hbm, og_hbm, w_hbm,
    dq_hbm, dk_hbm, dv_hbm,
    q_v, g_v, dq_v, og_v, pool_0, pool_1, stage, kv, acc, piece, came, running, total, home, stats,
    in_send, in_recv, pick_send, pick_recv, back_send, back_recv, home_send, home_recv,
    og_send, og_recv, self_in, self_move, load_sem, out_sem,
):
    me = lax.axis_index("seq")
    z = lax.axis_index("head")
    pool = (pool_0, pool_1)

    def remote(src, dst, send_sem, recv_sem, peer, peer_z=None):
        pltpu.make_async_remote_copy(
            src_ref=src, dst_ref=dst, send_sem=send_sem, recv_sem=recv_sem,
            device_id=(peer, z if peer_z is None else peer_z), device_id_type=MESH,
        ).start()

    def wait_for(ref, sem):
        pltpu.make_async_copy(ref, ref, sem).wait()

    loads = []

    def load(src, dst):
        copy = pltpu.make_async_copy(src, dst, load_sem.at[len(loads)])
        copy.start()
        loads.append(copy)

    load(og_hbm, og_v.at[z])
    for head in range(HEADS_HERE):
        load(q_hbm.at[:, head_cols(head)], q_v.at[head])
    for c in range(KV_HERE):
        for a, ref in enumerate((k_hbm, v_hbm)):
            load(ref.at[RUN - 1, :, :, head_cols(c)], kv.at[c, a, 0])

    barrier = pltpu.get_barrier_semaphore()

    def greet(t, carry):
        pl.semaphore_signal(
            barrier, inc=1, device_id=((me + t) % SEQ, z), device_id_type=MESH
        )
        return carry

    lax.fori_loop(1, SEQ, greet, 0)
    for t in range(1, ZDEV):
        pl.semaphore_signal(barrier, inc=1, device_id=(me, (z + t) % ZDEV), device_id_type=MESH)
    pl.semaphore_wait(barrier, SEQ - 1 + ZDEV - 1)

    for t in (1, 3, 2):
        remote(og_hbm, og_v.at[z], og_send, og_recv, me, (z + t) % ZDEV)

    def send_in(c, a):
        ref = (k_hbm, v_hbm)[a]
        pltpu.make_async_copy(
            ref.at[:, me, :, head_cols(c)], pool[c].at[a, pl.ds(me * RUN, RUN)], self_in.at[c, a]
        ).start()
        each_peer(
            me,
            lambda peer: remote(
                ref.at[:, peer, :, head_cols(c)],
                pool[c].at[a, pl.ds(me * RUN, RUN)],
                in_send.at[c], in_recv.at[c], peer,
            ),
        )

    def wait_in(c):
        others = pool[c].at[:, pl.ds(0, (SEQ - 1) * RUN)]
        wait_for(others, in_recv.at[c])
        wait_for(others, in_send.at[c])
        for a in range(2):
            wait_for(pool[c].at[a, pl.ds(0, RUN)], self_in.at[c, a])

    def send_picks(c):
        def choose(i, carry):
            for r in range(SLOTS):
                block = picks[i, r + 1]
                for a in range(2):
                    stage[c, i, a, r] = pool[c][a, block]
            return carry

        lax.fori_loop(0, SEQ, choose, 0)
        pltpu.make_async_copy(
            stage.at[c, me], kv.at[c, :, pl.ds(1, SLOTS), me], self_move.at[0, c]
        ).start()
        each_peer(
            me,
            lambda peer: remote(
                stage.at[c, peer], kv.at[c, :, pl.ds(1, SLOTS), me],
                pick_send.at[c], pick_recv.at[c], peer,
            ),
        )

    def wait_picks(c):
        others = stage.at[c, pl.ds(0, SEQ - 1)]
        wait_for(others, pick_recv.at[c])
        wait_for(others, pick_send.at[c])
        wait_for(stage.at[c, 0], self_move.at[0, c])

    def send_back(c):
        for slot in range(TOPK):
            for a in range(2):
                value = acc[a, slot]
                if a == 0:
                    value = value * FACTOR
                piece[c, a, slot] = value.astype(jnp.bfloat16).reshape(SEQ, PIECE, HEAD_DIM)
        pltpu.make_async_copy(
            piece.at[c, :, pl.ds(1, SLOTS), me], came.at[c, me], self_move.at[1, c]
        ).start()
        each_peer(
            me,
            lambda peer: remote(
                piece.at[c, :, pl.ds(1, SLOTS), peer], came.at[c, me],
                back_send.at[c], back_recv.at[c], peer,
            ),
        )

    def send_home(c):
        others = came.at[c, pl.ds(0, SEQ - 1)]
        wait_for(others, back_recv.at[c])
        wait_for(others, back_send.at[c])
        wait_for(came.at[c, 0], self_move.at[1, c])
        running[0] = jnp.zeros_like(running[0])

        def add(i, carry):
            for r in range(SLOTS):
                number = i * SLOTS + r
                running[number + 1] = (
                    came[c, i, :, r].astype(jnp.float32) + running[table[number]]
                )
            return carry

        lax.fori_loop(0, SEQ, add, 0)

        def gather(j, carry):
            for k in range(RUN):
                block = j * RUN + k
                total[c, :, block] = running[table[SEQ * SLOTS + block]].astype(jnp.bfloat16)
            return carry

        lax.fori_loop(0, SEQ, gather, 0)
        pltpu.make_async_copy(
            total.at[c, :, pl.ds(me * RUN, RUN)], home.at[c, :, :, me], self_move.at[2, c]
        ).start()
        each_peer(
            me,
            lambda peer: remote(
                total.at[c, :, pl.ds(peer * RUN, RUN)], home.at[c, :, :, me],
                home_send.at[c], home_recv.at[c], peer,
            ),
        )

    def finish(c):
        others = total.at[c, :, pl.ds(0, (SEQ - 1) * RUN)]
        wait_for(others, home_recv.at[c])
        wait_for(others, home_send.at[c])
        wait_for(total.at[c, :, pl.ds(0, RUN)], self_move.at[2, c])
        for a, ref in enumerate((dk_hbm, dv_hbm)):
            own = home[c, a, RUN - 1].astype(jnp.float32) + piece[c, a, 0].astype(jnp.float32)
            home[c, a, RUN - 1] = own.astype(jnp.bfloat16)
            pltpu.make_async_copy(
                home.at[c, a], ref.at[:, :, :, head_cols(c)], out_sem.at[c, a]
            ).start()

    send_in(0, 0)
    send_in(0, 1)
    send_in(1, 0)

    def project(w_v):
        w_load = pltpu.make_async_copy(w_hbm, w_v, load_sem.at[len(loads)])
        w_load.start()
        wait_in(0)
        send_picks(0)
        send_in(1, 1)
        w_load.wait()
        for copy in loads:
            copy.wait()
        og_others = og_v.at[pl.ds(0, ZDEV - 1)]
        wait_for(og_others, og_recv)
        wait_for(og_others, og_send)
        depth = og_v.shape[2]
        half = depth // 2
        for pair in range(HEADS_HERE // 2):
            rows = pl.ds(pair * 2 * HEAD_DIM, 2 * HEAD_DIM)

            def add(t, result, rows=rows):
                part = pl.ds(pl.multiple_of(t % 2 * half, half), half)
                columns = pl.ds(pl.multiple_of(t * half, half), half)
                return result + dot_nt(og_v[t // 2, :, part], w_v[rows, columns])

            result = lax.fori_loop(
                0, 2 * ZDEV, add, jnp.zeros((BLOCK, 2 * HEAD_DIM), jnp.float32)
            )
            for k in range(2):
                g_v[pair * 2 + k] = result[:, k * HEAD_DIM : (k + 1) * HEAD_DIM].astype(jnp.bfloat16)

    pl.run_scoped(project, pltpu.VMEM(w_hbm.shape, jnp.bfloat16))
    wait_picks(0)

    def attend(p_s, dp_s):
        def one_head(head, carry):
            c = head // GROUP

            @pl.when(head == 2)
            def _():
                wait_in(1)
                send_picks(1)

            @pl.when(head == GROUP)
            def _():
                send_back(0)
                wait_picks(1)

            @pl.when(head == GROUP + 2)
            def _():
                send_home(0)

            @pl.when(head % GROUP == 0)
            def _():
                acc[...] = jnp.zeros_like(acc)

            query = q_v[head]
            grad = g_v[head]

            def tiles(slot):
                key = kv[c, 0, slot].reshape(BLOCK, HEAD_DIM)
                value = kv[c, 1, slot].reshape(BLOCK, HEAD_DIM)
                return key, value

            def forward(slot, state):
                key, value = tiles(slot)
                scores = dot_nt(key, query)
                if state is None:
                    key_at = lax.broadcasted_iota(jnp.int32, (BLOCK, BLOCK), 0)
                    query_at = lax.broadcasted_iota(jnp.int32, (BLOCK, BLOCK), 1)
                    scores = jnp.where(key_at <= query_at, scores, -jnp.inf)
                    top = jnp.max(scores, axis=0, keepdims=True)
                else:
                    top = jnp.maximum(state[0], jnp.max(scores, axis=0, keepdims=True))
                shifted = jnp.exp2((scores - top) * EXP2_SCALE)
                grad_weights = dot_nt(value, grad)
                p_s[slot] = shifted
                dp_s[slot] = grad_weights
                stats[slot] = top
                norm = jnp.sum(shifted, axis=0, keepdims=True)
                row_dot = jnp.sum(shifted * grad_weights, axis=0, keepdims=True)
                if state is not None:
                    shrink = jnp.exp2((state[0] - top) * EXP2_SCALE)
                    norm = norm + state[1] * shrink
                    row_dot = row_dot + state[2] * shrink
                return top, norm, row_dot

            state = forward(0, None)
            top, norm, row_dot = lax.fori_loop(1, TOPK, forward, state)
            inverse = 1.0 / norm
            row_dot = row_dot * inverse

            def backward(slot, query_part):
                key, _ = tiles(slot)
                weights = p_s[slot] * (jnp.exp2((stats[slot] - top) * EXP2_SCALE) * inverse)
                weights_low = weights.astype(jnp.bfloat16)
                grad_low = (weights * (dp_s[slot] - row_dot)).astype(jnp.bfloat16)
                acc[1, slot] += dot_nn(weights_low, grad)
                acc[0, slot] += dot_nn(grad_low, query)
                return query_part + dot_tn(key, grad_low)

            query_part = lax.fori_loop(
                0, TOPK, backward, jnp.zeros((HEAD_DIM, BLOCK), jnp.float32)
            )
            dq_v[head] = jnp.transpose(query_part * FACTOR).astype(jnp.bfloat16)
            return carry

        lax.fori_loop(0, HEADS_HERE, one_head, 0)

    pl.run_scoped(
        attend,
        pltpu.VMEM((TOPK, BLOCK, BLOCK), jnp.float32),
        pltpu.VMEM((TOPK, BLOCK, BLOCK), jnp.float32),
    )
    send_back(1)
    outs = []
    for head in range(HEADS_HERE):
        copy = pltpu.make_async_copy(
            dq_v.at[head], dq_hbm.at[:, head_cols(head)], load_sem.at[head]
        )
        copy.start()
        outs.append(copy)
    send_home(1)
    finish(0)
    finish(1)
    for copy in outs:
        copy.wait()
    for c in range(KV_HERE):
        for a, ref in enumerate((dk_hbm, dv_hbm)):
            pltpu.make_async_copy(
                home.at[c, a], ref.at[:, :, :, head_cols(c)], out_sem.at[c, a]
            ).wait()


def shards(queries, keys, values, out_grad, out_weight, selected):
    bf16, f32 = jnp.bfloat16, jnp.float32
    kv_cols = keys.shape[1]
    tiled = (RUN, SEQ, PIECE, kv_cols)
    listed = selected[:, 1:].reshape(-1)
    count = listed.shape[0]
    numbers = jnp.arange(count, dtype=jnp.int32)
    target = jnp.concatenate([listed, jnp.arange(KBLOCKS, dtype=jnp.int32)])
    limit = jnp.concatenate([numbers, jnp.full((KBLOCKS,), count, jnp.int32)])
    same = (target[:, None] == listed[None, :]) & (numbers[None, :] < limit[:, None])
    table = jnp.max(jnp.where(same, numbers[None, :] + 1, 0), axis=1)
    tile = (PIECE, HEAD_DIM)
    dma = pltpu.SemaphoreType.DMA
    hbm = pl.BlockSpec(memory_space=pltpu.HBM)
    smem = pl.BlockSpec(memory_space=pltpu.SMEM)
    query_grad, key_grad, value_grad = pl.pallas_call(
        kernel,
        out_shape=(
            jax.ShapeDtypeStruct(queries.shape, bf16),
            jax.ShapeDtypeStruct(tiled, bf16),
            jax.ShapeDtypeStruct(tiled, bf16),
        ),
        in_specs=[smem, smem, hbm, hbm, hbm, hbm, hbm],
        out_specs=(hbm, hbm, hbm),
        scratch_shapes=[
            pltpu.VMEM((HEADS_HERE, BLOCK, HEAD_DIM), bf16),
            pltpu.VMEM((HEADS_HERE, BLOCK, HEAD_DIM), bf16),
            pltpu.VMEM((HEADS_HERE, BLOCK, HEAD_DIM), bf16),
            pltpu.VMEM((ZDEV, *out_grad.shape), bf16),
            *[pltpu.VMEM((2, KBLOCKS, *tile), bf16)] * KV_HERE,
            pltpu.VMEM((KV_HERE, SEQ, 2, SLOTS, *tile), bf16),
            pltpu.VMEM((KV_HERE, 2, TOPK, SEQ, *tile), bf16),
            pltpu.VMEM((2, TOPK, BLOCK, HEAD_DIM), f32),
            pltpu.VMEM((KV_HERE, 2, TOPK, SEQ, *tile), bf16),
            pltpu.VMEM((KV_HERE, SEQ, 2, SLOTS, *tile), bf16),
            pltpu.VMEM((SEQ * SLOTS + 1, 2, *tile), f32),
            pltpu.VMEM((KV_HERE, 2, KBLOCKS, *tile), bf16),
            pltpu.VMEM((KV_HERE, 2, RUN, SEQ, *tile), bf16),
            pltpu.VMEM((TOPK, 1, BLOCK), f32),
            *[dma((KV_HERE,))] * 8,
            dma, dma,
            dma((KV_HERE, 2)),
            dma((3, KV_HERE)),
            dma((HEADS_HERE + 6,)),
            dma((KV_HERE, 2)),
        ],
        compiler_params=pltpu.CompilerParams(
            collective_id=0, has_side_effects=True, vmem_limit_bytes=62 << 20
        ),
    )(
        selected, table, queries, keys.reshape(tiled), values.reshape(tiled), out_grad, out_weight
    )
    return query_grad, key_grad.reshape(keys.shape), value_grad.reshape(values.shape)


def solution(mesh):
    in_specs = (
        P("seq", "head"),
        P("seq", "head"),
        P("seq", "head"),
        P("seq", "head"),
        P("head", None),
        P(),
    )
    out_specs = (P("seq", "head"), P("seq", "head"), P("seq", "head"))
    return jax.shard_map(shards, mesh=mesh, in_specs=in_specs, out_specs=out_specs, check_vma=False)
```

time: 439 us -> 198 us (0.45)
  Pallas kernels: 0 us -> 188 us
  matrix products: 142 us -> 0 us
  blocking collectives: 98.5 us -> 0 us
  waiting for transfers between devices: 81.6 us -> 0 us
  other arithmetic: 46 us -> 1.49 us
  local copies, waits for them, and re-layouts: 39.5 us -> 8.34 us
  starting transfers between devices: 15.9 us -> 0 us
  between operations: 14.2 us -> 0.67 us
    pallas_call x0 -> x1, Pallas kernels: none -> 188 us  [shards(): pl.pallas_call(kernel, out_shape=(jax.ShapeDtypeStruct(queries.shape, bf1...]
    dot_general x51 -> x0, matrix products: 142 us -> none  [the longest x8 34.3 us: one_head(): jnp.dot(weights_low, value_head, preferred_element_type=jnp.float32)]
    all_to_all x2 -> x0, blocking collectives: 98.5 us -> none  [in_one_piece(): lax.all_to_all(both, axis, split_axis=split_dim, concat_axis=concat_dim,...]
    all_to_all x2 -> x0, waiting for transfers between devices: 80.9 us -> none  [in_one_piece(): lax.all_to_all(both, axis, split_axis=split_dim, concat_axis=concat_dim,...]
    div x8 -> x0, other arithmetic: 31.5 us -> none  [one_head(): weights = shifted / jnp.sum(shifted, axis=1, keepdims=True)]
    all_to_all x2 -> x0, starting transfers between devices: 15.9 us -> none  [in_one_piece(): lax.all_to_all(both, axis, split_axis=split_dim, concat_axis=concat_dim,...]
    dynamic_slice x16 -> x0, local copies, waits for them, and re-layouts: 8.21 us -> none  [one_head(): lax.dynamic_slice_in_dim(grad_output, head_index * HEAD_DIM, HEAD_DIM, 1)]
    reduce_sum x8 -> x0, other arithmetic: 7.95 us -> none  [one_head(): weights = shifted / jnp.sum(shifted, axis=1, keepdims=True)]
  transfers between devices with their start and end apart: 3 -> 0, of which waited for: 2 -> 0; matrix products, arithmetic and copies ran while one was open for 5% -> 0% of each run, Pallas kernels for 0% -> 0%
where the time goes in v1:
time: 198 us
  Pallas kernels  188 us (95%)
  local copies, waits for them, and re-layouts  8.34 us (4%)
    pallas_call x1, Pallas kernels, shards(): pl.pallas_call(kernel, out_shape=(jax.ShapeDtypeStruct(queries.shape, bf1...  188 us
    unnamed x8, local copies, waits for them, and re-layouts  7.45 us

profile of v1, /device:TPU:1, one launch (start us, length us, event | category | flops | bytes accessed | tf_op | source)
XLA Modules:
  0.0 198.1 jit_solution(11243946650279543256)
XLA Ops:
  0.6 0.7 slice.3
  1.3 0.1 copy.12
  1.4 0.1 reshape.29
  1.5 0.1 pad_add_fusion
  1.6 1.4 select_reduce_fusion.table
  3.0 1.4 copy.13.picks
  4.4 187.6 %shard_map.85 = (bf16[512,1024]{1,0:T(8,128)(2,1)}, bf16[8,32,16,256]{3,2,1,0:T(8,128)(2,1)}, bf16[8,32,16,256]{3,2,1,0:T(8,128)(2,1)}) custom-call(s32[32,6]{1,0:T(8,128)} %copy.13.picks, s32[416]{0:T(512)} %select_reduce_fusion.table, bf16[512,1024]{1,0:T(8,128)(2,1)} %q_hbm.1, bf16[8,32,16,256]{3,2,1,0:T(8,128)(2,1)} %bitcast.4, ...), custom_call_target="tpu_custom_call" | custom-call | tf_op jit(solution)/shard_map/pallas_call | solution.py:382
  192.0 0.0 copy-start.1
  192.0 2.4 %copy.17 = bf16[512,1024]{1,0:T(8,128)(2,1)} copy(bf16[512,1024]{1,0:T(8,128)(2,1)} %get-tuple-element.12) | data formatting | bytes 2097152
  194.4 0.0 copy-done.1
  194.4 0.0 copy-start
  194.4 1.3 copy.18
  195.7 1.0 copy-done
  196.7 1.3 copy.19
  (2 shorter events, 0.0 us)
Async XLA Ops:
  192.0 2.4 %copy-start.1 = (bf16[8,32,16,256]{3,2,1,0:T(8,128)(2,1)S(1)}, bf16[8,32,16,256]{3,2,1,0:T(8,128)(2,1)}, u32[]{:S(2)}) copy-start(bf16[8,32,16,256]{3,2,1,0:T(8,128)(2,1)} %get-tuple-element.7) | copy-start | bytes 6291460
  194.4 2.3 %copy-start = (bf16[8,32,16,256]{3,2,1,0:T(8,128)(2,1)S(1)}, bf16[8,32,16,256]{3,2,1,0:T(8,128)(2,1)}, u32[]{:S(2)}) copy-start(bf16[8,32,16,256]{3,2,1,0:T(8,128)(2,1)} %get-tuple-element.8) | copy-start | bytes 6291460

commit v2 on v1

v2 whole, which is shorter than its diff:
```python
import functools
import math

import jax
import jax.numpy as jnp
from jax import lax
from jax.experimental import pallas as pl
from jax.experimental.pallas import tpu as pltpu
from jax.sharding import PartitionSpec as P

HEAD_DIM = 128
BLOCK = 512
TOPK = 6
SEQ = 32
ZDEV = 4
RUN = 8
PIECE = BLOCK // SEQ
SLOTS = TOPK - 1
KBLOCKS = SEQ * RUN
TABLE = 512
HEADS_HERE = 8
KV_HERE = 2
GROUP = HEADS_HERE // KV_HERE
FACTOR = HEAD_DIM**-0.5
EXP2_SCALE = FACTOR * math.log2(math.e)
MESH = pl.DeviceIdType.MESH

OFFSETS = [
    (1, 0), (3, 0), (0, 1), (0, 3), (1, 1), (3, 3), (1, 3), (3, 1),
    (2, 0), (0, 2), (1, 2), (3, 2), (2, 1), (2, 3), (2, 2),
]
DX_CODE = sum(dx * 4**t for t, (dx, _) in enumerate(OFFSETS))
DY_CODE = sum(dy * 4**t for t, (_, dy) in enumerate(OFFSETS))


def each_peer(me, visit):
    x, y, core = me // 8, me // 2 % 4, me % 2

    def step(flip, codes):
        dx_code, dy_code = codes
        peer = (x + dx_code % 4) % 4 * 8 + (y + dy_code % 4) % 4 * 2 + (core + flip) % 2
        visit(peer)
        return dx_code // 4, dy_code // 4

    for flip in (0, 1):
        lax.fori_loop(
            0,
            len(OFFSETS),
            lambda t, codes, flip=flip: step(flip, codes),
            (jnp.int32(DX_CODE), jnp.int32(DY_CODE)),
        )
    visit(x * 8 + y * 2 + 1 - core)


def dot_nt(a, b):
    return lax.dot_general(a, b, (((1,), (1,)), ((), ())), preferred_element_type=jnp.float32)


def dot_nn(a, b):
    return jnp.dot(a, b, preferred_element_type=jnp.float32)


def dot_tn(a, b):
    return lax.dot_general(a, b, (((0,), (0,)), ((), ())), preferred_element_type=jnp.float32)


def head_cols(index):
    return pl.ds(index * HEAD_DIM, HEAD_DIM)


def kernel(
    selected, q_hbm, k_hbm, v_hbm, og_hbm, w_hbm,
    dq_out, dk_out, dv_out,
    selected_v, table_v, table, q_v, g_v, og_v, pool_0, pool_1, pool_2, pool_3, stage, kv, acc, piece, came,
    running, total, stats,
    in_send, in_recv, pick_send, pick_recv, back_send, back_recv, home_send, home_recv,
    og_send, og_recv, self_move, load_sem, table_sem,
):
    me = lax.axis_index("seq")
    z = lax.axis_index("head")
    pool = ((pool_0, pool_1), (pool_2, pool_3))

    def remote(src, dst, send_sem, recv_sem, peer, peer_z=None):
        pltpu.make_async_remote_copy(
            src_ref=src, dst_ref=dst, send_sem=send_sem, recv_sem=recv_sem,
            device_id=(peer, z if peer_z is None else peer_z), device_id_type=MESH,
        ).start()

    def wait_for(ref, sem):
        pltpu.make_async_copy(ref, ref, sem).wait()

    table_load = pltpu.make_async_copy(selected, selected_v, table_sem)
    table_load.start()
    loads = []

    def load(src, dst):
        copy = pltpu.make_async_copy(src, dst, load_sem.at[len(loads)])
        copy.start()
        loads.append(copy)

    load(og_hbm, og_v.at[z])
    for head in range(HEADS_HERE):
        load(q_hbm.at[:, head_cols(head)], q_v.at[head])
    for c in range(KV_HERE):
        for a, ref in enumerate((k_hbm, v_hbm)):
            load(ref.at[RUN - 1, :, :, head_cols(c)], kv.at[c, a, 0])

    barrier = pltpu.get_barrier_semaphore()

    def greet(t, carry):
        pl.semaphore_signal(
            barrier, inc=1, device_id=((me + t) % SEQ, z), device_id_type=MESH
        )
        return carry

    lax.fori_loop(1, SEQ, greet, 0)
    for t in range(1, ZDEV):
        pl.semaphore_signal(barrier, inc=1, device_id=(me, (z + t) % ZDEV), device_id_type=MESH)
    pl.semaphore_wait(barrier, SEQ - 1 + ZDEV - 1)

    above, below = (z + 1) % ZDEV, (z + ZDEV - 1) % ZDEV
    remote(og_hbm, og_v.at[z], og_send.at[0], og_recv.at[0], me, above)
    remote(og_hbm, og_v.at[z], og_send.at[1], og_recv.at[1], me, below)

    def relay_cotangent():
        half = og_v.shape[1] // 2
        for way, (source, target) in enumerate(((below, above), (above, below))):
            wait_for(og_v.at[source], og_recv.at[way])
            part = og_v.at[source, pl.ds(way * half, half)]
            remote(part, part, og_send.at[2 + way], og_recv.at[2 + way], me, target)

    def wait_cotangent():
        half = og_v.at[0, pl.ds(0, og_v.shape[1] // 2)]
        for way in range(2):
            wait_for(og_v.at[0], og_send.at[way])
            wait_for(half, og_send.at[2 + way])
            wait_for(half, og_recv.at[2 + way])

    def send_in(c, a):
        ref = (k_hbm, v_hbm)[a]
        mine = pool[c][a].at[pl.ds(me * RUN, RUN)]
        pltpu.make_async_copy(
            ref.at[:, me, :, head_cols(c)], mine, self_move.at[0, c, a]
        ).start()
        each_peer(
            me,
            lambda peer: remote(
                ref.at[:, peer, :, head_cols(c)], mine,
                in_send.at[c, a], in_recv.at[c, a], peer,
            ),
        )

    def send_picks(c, a):
        others = pool[c][a].at[pl.ds(0, (SEQ - 1) * RUN)]
        wait_for(others, in_recv.at[c, a])
        wait_for(others, in_send.at[c, a])
        wait_for(pool[c][a].at[pl.ds(0, RUN)], self_move.at[0, c, a])

        def choose(i, carry):
            for r in range(SLOTS):
                stage[c, a, i, r] = pool[c][a][table[0, i * SLOTS + r]]
            return carry

        lax.fori_loop(0, SEQ, choose, 0)
        mine = kv.at[c, a, pl.ds(1, SLOTS), me]
        pltpu.make_async_copy(stage.at[c, a, me], mine, self_move.at[1, c, a]).start()
        each_peer(
            me,
            lambda peer: remote(
                stage.at[c, a, peer], mine, pick_send.at[c, a], pick_recv.at[c, a], peer
            ),
        )

    def wait_picks(c, a):
        others = stage.at[c, a, pl.ds(0, SEQ - 1)]
        wait_for(others, pick_recv.at[c, a])
        wait_for(others, pick_send.at[c, a])
        wait_for(stage.at[c, a, 0], self_move.at[1, c, a])

    def send_back(c, a):
        for slot in range(TOPK):
            value = acc[a, slot]
            if a == 0:
                value = value * FACTOR
            piece[c, a, slot] = value.astype(jnp.bfloat16).reshape(SEQ, PIECE, HEAD_DIM)
        mine = came.at[c, a, me]
        pltpu.make_async_copy(
            piece.at[c, a, pl.ds(1, SLOTS), me], mine, self_move.at[2, c, a]
        ).start()
        each_peer(
            me,
            lambda peer: remote(
                piece.at[c, a, pl.ds(1, SLOTS), peer], mine,
                back_send.at[c, a], back_recv.at[c, a], peer,
            ),
        )

    def send_home(c, a):
        others = came.at[c, a, pl.ds(0, SEQ - 1)]
        wait_for(others, back_recv.at[c, a])
        wait_for(others, back_send.at[c, a])
        wait_for(came.at[c, a, 0], self_move.at[2, c, a])
        running[0] = jnp.zeros_like(running[0])

        def add(i, carry):
            for r in range(SLOTS):
                number = i * SLOTS + r
                running[number + 1] = (
                    came[c, a, i, r].astype(jnp.float32) + running[table[1, number]]
                )
            return carry

        lax.fori_loop(0, SEQ, add, 0)

        def gather(j, carry):
            for k in range(RUN):
                block = j * RUN + k
                total[c, a, block] = running[table[1, SEQ * SLOTS + block]].astype(jnp.bfloat16)
            return carry

        lax.fori_loop(0, SEQ, gather, 0)
        mine = (dk_out, dv_out)[a].at[:, me, :, head_cols(c)]
        pltpu.make_async_copy(
            total.at[c, a, pl.ds(me * RUN, RUN)], mine, self_move.at[3, c, a]
        ).start()
        each_peer(
            me,
            lambda peer: remote(
                total.at[c, a, pl.ds(peer * RUN, RUN)], mine,
                home_send.at[c, a], home_recv.at[c, a], peer,
            ),
        )

    def finish(c, a):
        others = total.at[c, a, pl.ds(0, (SEQ - 1) * RUN)]
        wait_for(others, home_recv.at[c, a])
        wait_for(others, home_send.at[c, a])
        wait_for(total.at[c, a, pl.ds(0, RUN)], self_move.at[3, c, a])
        ref, columns = (dk_out, dv_out)[a], head_cols(c)
        own = ref[RUN - 1, :, :, columns].astype(jnp.float32)
        own = own + piece[c, a, 0].astype(jnp.float32)
        ref[RUN - 1, :, :, columns] = own.astype(jnp.bfloat16)

    def make_table():
        table_load.wait()
        rows_of = jnp.transpose(selected_v[...])
        lane = lax.broadcasted_iota(jnp.int32, (SEQ, table_v.shape[1]), 1)
        row = lax.broadcasted_iota(jnp.int32, (SEQ, table_v.shape[1]), 0)
        count = SEQ * SLOTS
        listed = jnp.zeros_like(lane)
        for r in range(SLOTS):
            listed += jnp.where(lane == row * SLOTS + r, rows_of[:, r + 1 : r + 2], 0)
        listed = jnp.sum(listed, axis=0, keepdims=True)
        target = jnp.where(lane < count, listed, lane - count)
        limit = jnp.minimum(lane, count)
        latest = jnp.zeros_like(lane)
        for r in range(SLOTS):
            number = row * SLOTS + r
            same = (rows_of[:, r + 1 : r + 2] == target) & (number < limit)
            latest = jnp.maximum(latest, jnp.where(same, number + 1, 0))
        table_v[0:1, :] = listed
        table_v[1:2, :] = jnp.max(latest, axis=0, keepdims=True)
        table_store = pltpu.make_async_copy(table_v, table, table_sem)
        table_store.start()
        table_store.wait()

    send_in(0, 0)
    send_in(0, 1)
    make_table()

    def project(w_v):
        w_load = pltpu.make_async_copy(w_hbm, w_v, load_sem.at[len(loads)])
        w_load.start()
        send_picks(0, 0)
        relay_cotangent()
        send_picks(0, 1)
        send_in(1, 0)
        send_in(1, 1)
        w_load.wait()
        for copy in loads:
            copy.wait()
        wait_cotangent()
        depth = og_v.shape[2]
        half = depth // 2
        for pair in range(HEADS_HERE // 2):
            rows = pl.ds(pair * 2 * HEAD_DIM, 2 * HEAD_DIM)

            def add(t, result, rows=rows):
                part = pl.ds(pl.multiple_of(t % 2 * half, half), half)
                columns = pl.ds(pl.multiple_of(t * half, half), half)
                return result + dot_nt(og_v[t // 2, :, part], w_v[rows, columns])

            result = lax.fori_loop(
                0, 2 * ZDEV, add, jnp.zeros((BLOCK, 2 * HEAD_DIM), jnp.float32)
            )
            for k in range(2):
                g_v[pair * 2 + k] = result[:, k * HEAD_DIM : (k + 1) * HEAD_DIM].astype(jnp.bfloat16)

    pl.run_scoped(project, pltpu.VMEM(w_hbm.shape, jnp.bfloat16))
    wait_picks(0, 0)
    wait_picks(0, 1)

    def attend(p_s, dp_s):
        def one_head(head, carry):
            c = head // GROUP

            @pl.when(head == 1)
            def _():
                send_picks(1, 0)

            @pl.when(head == 3)
            def _():
                send_picks(1, 1)

            @pl.when(head == GROUP)
            def _():
                send_back(0, 0)
                send_back(0, 1)
                wait_picks(1, 0)
                wait_picks(1, 1)

            @pl.when(head == GROUP + 1)
            def _():
                send_home(0, 0)

            @pl.when(head == GROUP + 2)
            def _():
                send_home(0, 1)

            @pl.when(head % GROUP == 0)
            def _():
                acc[...] = jnp.zeros_like(acc)

            query = q_v[head]
            grad = g_v[head]

            def tiles(slot):
                key = kv[c, 0, slot].reshape(BLOCK, HEAD_DIM)
                value = kv[c, 1, slot].reshape(BLOCK, HEAD_DIM)
                return key, value

            def forward(slot, state):
                key, value = tiles(slot)
                scores = dot_nt(key, query)
                if state is None:
                    key_at = lax.broadcasted_iota(jnp.int32, (BLOCK, BLOCK), 0)
                    query_at = lax.broadcasted_iota(jnp.int32, (BLOCK, BLOCK), 1)
                    scores = jnp.where(key_at <= query_at, scores, -jnp.inf)
                    top = jnp.max(scores, axis=0, keepdims=True)
                else:
                    top = jnp.maximum(state[0], jnp.max(scores, axis=0, keepdims=True))
                shifted = jnp.exp2((scores - top) * EXP2_SCALE)
                grad_weights = dot_nt(value, grad)
                p_s[slot] = shifted
                dp_s[slot] = grad_weights
                stats[slot] = top
                norm = jnp.sum(shifted, axis=0, keepdims=True)
                row_dot = jnp.sum(shifted * grad_weights, axis=0, keepdims=True)
                if state is not None:
                    shrink = jnp.exp2((state[0] - top) * EXP2_SCALE)
                    norm = norm + state[1] * shrink
                    row_dot = row_dot + state[2] * shrink
                return top, norm, row_dot

            state = forward(0, None)
            top, norm, row_dot = lax.fori_loop(1, TOPK, forward, state)
            inverse = 1.0 / norm
            row_dot = row_dot * inverse

            def backward(slot, query_part):
                key, _ = tiles(slot)
                weights = p_s[slot] * (jnp.exp2((stats[slot] - top) * EXP2_SCALE) * inverse)
                weights_low = weights.astype(jnp.bfloat16)
                grad_low = (weights * (dp_s[slot] - row_dot)).astype(jnp.bfloat16)
                acc[1, slot] += dot_nn(weights_low, grad)
                acc[0, slot] += dot_nn(grad_low, query)
                return query_part + dot_tn(key, grad_low)

            query_part = lax.fori_loop(
                0, TOPK, backward, jnp.zeros((HEAD_DIM, BLOCK), jnp.float32)
            )
            columns = pl.ds(pl.multiple_of(head * HEAD_DIM, HEAD_DIM), HEAD_DIM)
            dq_out[:, columns] = jnp.transpose(query_part * FACTOR).astype(jnp.bfloat16)
            return carry

        lax.fori_loop(0, HEADS_HERE, one_head, 0)

    pl.run_scoped(
        attend,
        pltpu.VMEM((TOPK, BLOCK, BLOCK), jnp.float32),
        pltpu.VMEM((TOPK, BLOCK, BLOCK), jnp.float32),
    )
    send_back(1, 0)
    send_back(1, 1)
    send_home(1, 0)
    send_home(1, 1)
    for c in range(KV_HERE):
        for a in range(2):
            finish(c, a)


def shards(queries, keys, values, out_grad, out_weight, selected):
    bf16, f32 = jnp.bfloat16, jnp.float32
    kv_cols = keys.shape[1]
    tiled = (RUN, SEQ, PIECE, kv_cols)
    tile = (PIECE, HEAD_DIM)
    dma = pltpu.SemaphoreType.DMA
    hbm = pl.BlockSpec(memory_space=pltpu.HBM)
    vmem = pl.BlockSpec(memory_space=pltpu.VMEM)
    query_grad, key_grad, value_grad = pl.pallas_call(
        kernel,
        out_shape=(
            jax.ShapeDtypeStruct(queries.shape, bf16),
            jax.ShapeDtypeStruct(tiled, bf16),
            jax.ShapeDtypeStruct(tiled, bf16),
        ),
        in_specs=[hbm] * 6,
        out_specs=(vmem, vmem, vmem),
        scratch_shapes=[
            pltpu.VMEM(selected.shape[::-1], jnp.int32),
            pltpu.VMEM((2, TABLE), jnp.int32),
            pltpu.SMEM((2, TABLE), jnp.int32),
            pltpu.VMEM((HEADS_HERE, BLOCK, HEAD_DIM), bf16),
            pltpu.VMEM((HEADS_HERE, BLOCK, HEAD_DIM), bf16),
            pltpu.VMEM((ZDEV, *out_grad.shape), bf16),
            *[pltpu.VMEM((KBLOCKS, *tile), bf16)] * 2 * KV_HERE,
            pltpu.VMEM((KV_HERE, 2, SEQ, SLOTS, *tile), bf16),
            pltpu.VMEM((KV_HERE, 2, TOPK, SEQ, *tile), bf16),
            pltpu.VMEM((2, TOPK, BLOCK, HEAD_DIM), f32),
            pltpu.VMEM((KV_HERE, 2, TOPK, SEQ, *tile), bf16),
            pltpu.VMEM((KV_HERE, 2, SEQ, SLOTS, *tile), bf16),
            pltpu.VMEM((SEQ * SLOTS + 1, *tile), f32),
            pltpu.VMEM((KV_HERE, 2, KBLOCKS, *tile), bf16),
            pltpu.VMEM((TOPK, 1, BLOCK), f32),
            *[dma((KV_HERE, 2))] * 8,
            dma((4,)),
            dma((4,)),
            dma((4, KV_HERE, 2)),
            dma((HEADS_HERE + 6,)),
            dma,
        ],
        compiler_params=pltpu.CompilerParams(
            collective_id=0, has_side_effects=True, vmem_limit_bytes=62 << 20
        ),
    )(
        selected.T, queries, keys.reshape(tiled), values.reshape(tiled), out_grad, out_weight
    )
    return query_grad, key_grad.reshape(keys.shape), value_grad.reshape(values.shape)


def solution(mesh):
    in_specs = (
        P("seq", "head"),
        P("seq", "head"),
        P("seq", "head"),
        P("seq", "head"),
        P("head", None),
        P(),
    )
    out_specs = (P("seq", "head"), P("seq", "head"), P("seq", "head"))
    return jax.shard_map(shards, mesh=mesh, in_specs=in_specs, out_specs=out_specs, check_vma=False)
```

time: 198 us -> 175 us (0.88)
  Pallas kernels: 188 us -> 168 us
  local copies, waits for them, and re-layouts: 8.34 us -> 6.08 us
    pallas_call x1, Pallas kernels: 188 us -> 168 us  [shards(): pl.pallas_call(kernel, out_shape=(jax.ShapeDtypeStruct(queries.shape, bf1...]
    unnamed x8 -> x7, local copies, waits for them, and re-layouts: 7.45 us -> 6.08 us
where the time goes in v2:
time: 175 us
  Pallas kernels  168 us (96%)
  local copies, waits for them, and re-layouts  6.08 us (3%)
    pallas_call x1, Pallas kernels, shards(): pl.pallas_call(kernel, out_shape=(jax.ShapeDtypeStruct(queries.shape, bf1...  168 us
    unnamed x7, local copies, waits for them, and re-layouts  6.08 us

profile of v2, /device:TPU:1, one launch (start us, length us, event | category | flops | bytes accessed | tf_op | source)
XLA Modules:
  0.0 174.7 jit_solution(4760631133024908731)
XLA Ops:
  0.6 168.0 %shard_map.85 = (bf16[512,1024]{1,0:T(8,128)(2,1)}, bf16[8,32,16,256]{3,2,1,0:T(8,128)(2,1)}, bf16[8,32,16,256]{3,2,1,0:T(8,128)(2,1)}) custom-call(s32[6,32]{1,0:T(8,128)} %bitcast.9, bf16[512,1024]{1,0:T(8,128)(2,1)} %q_hbm.1, bf16[8,32,16,256]{3,2,1,0:T(8,128)(2,1)} %bitcast.7, bf16[8,32,16,256]{3,2,1,0:T(8,128)(2,1)} %bitcast.8, ...), custom_call_target="tpu_custom_call" | custom-call | tf_op jit(solution)/shard_map/pallas_call | solution.py:410
  168.6 0.0 copy-start.1
  168.6 2.4 %copy.12 = bf16[512,1024]{1,0:T(8,128)(2,1)} copy(bf16[512,1024]{1,0:T(8,128)(2,1)} %get-tuple-element.12) | data formatting | bytes 2097152
  171.0 0.0 copy-done.1
  171.0 0.0 copy-start
  171.0 1.3 copy.13
  172.4 1.0 copy-done
  173.4 1.3 copy.14
Async XLA Ops:
  168.6 2.4 %copy-start.1 = (bf16[8,32,16,256]{3,2,1,0:T(8,128)(2,1)S(1)}, bf16[8,32,16,256]{3,2,1,0:T(8,128)(2,1)}, u32[]{:S(2)}) copy-start(bf16[8,32,16,256]{3,2,1,0:T(8,128)(2,1)} %get-tuple-element.7) | copy-start | bytes 6291460
  171.0 2.3 %copy-start = (bf16[8,32,16,256]{3,2,1,0:T(8,128)(2,1)S(1)}, bf16[8,32,16,256]{3,2,1,0:T(8,128)(2,1)}, u32[]{:S(2)}) copy-start(bf16[8,32,16,256]{3,2,1,0:T(8,128)(2,1)} %get-tuple-element.8) | copy-start | bytes 6291460

commit v3 on v2

--- a/solution.py
+++ b/solution.py
@@ -26,8 +26,8 @@
 MESH = pl.DeviceIdType.MESH
 
 OFFSETS = [
-    (1, 0), (3, 0), (0, 1), (0, 3), (1, 1), (3, 3), (1, 3), (3, 1),
-    (2, 0), (0, 2), (1, 2), (3, 2), (2, 1), (2, 3), (2, 2),
+    (2, 2), (1, 2), (2, 1), (3, 2), (2, 3), (1, 1), (3, 3), (1, 3),
+    (3, 1), (2, 0), (0, 2), (1, 0), (3, 0), (0, 1), (0, 3),
 ]
 DX_CODE = sum(dx * 4**t for t, (dx, _) in enumerate(OFFSETS))
 DY_CODE = sum(dy * 4**t for t, (_, dy) in enumerate(OFFSETS))
@@ -47,7 +47,7 @@
             0,
             len(OFFSETS),
             lambda t, codes, flip=flip: step(flip, codes),
-            (jnp.int32(DX_CODE), jnp.int32(DY_CODE)),
+            (DX_CODE + core * (DY_CODE - DX_CODE), DY_CODE + core * (DX_CODE - DY_CODE)),
         )
     visit(x * 8 + y * 2 + 1 - core)
 
@@ -376,9 +376,9 @@
                 acc[0, slot] += dot_nn(grad_low, query)
                 return query_part + dot_tn(key, grad_low)
 
-            query_part = lax.fori_loop(
-                0, TOPK, backward, jnp.zeros((HEAD_DIM, BLOCK), jnp.float32)
-            )
+            query_part = jnp.zeros((HEAD_DIM, BLOCK), jnp.float32)
+            for slot in range(TOPK):
+                query_part = backward(slot, query_part)
             columns = pl.ds(pl.multiple_of(head * HEAD_DIM, HEAD_DIM), HEAD_DIM)
             dq_out[:, columns] = jnp.transpose(query_part * FACTOR).astype(jnp.bfloat16)
             return carry
@@ -410,9 +410,9 @@
     query_grad, key_grad, value_grad = pl.pallas_call(
         kernel,
         out_shape=(
-            jax.ShapeDtypeStruct(queries.shape, bf16),
-            jax.ShapeDtypeStruct(tiled, bf16),
-            jax.ShapeDtypeStruct(tiled, bf16),
+            pltpu.VMEM(queries.shape, bf16),
+            pltpu.VMEM(tiled, bf16),
+            pltpu.VMEM(tiled, bf16),
         ),
         in_specs=[hbm] * 6,
         out_specs=(vmem, vmem, vmem),
@@ -440,7 +440,7 @@
             dma,
         ],
         compiler_params=pltpu.CompilerParams(
-            collective_id=0, has_side_effects=True, vmem_limit_bytes=62 << 20
+            collective_id=0, has_side_effects=True, vmem_limit_bytes=56 << 20
         ),
     )(
         selected.T, queries, keys.reshape(tiled), values.reshape(tiled), out_grad, out_weight

time: 175 us -> 164 us (0.937)
  Pallas kernels: 168 us -> 160 us
  local copies, waits for them, and re-layouts: 6.08 us -> 3.61 us
    pallas_call x1, Pallas kernels: 168 us -> 160 us  [shards(): pl.pallas_call(kernel, out_shape=(pltpu.VMEM(queries.shape, bf16), pltpu....]
    unnamed x7 -> x3, local copies, waits for them, and re-layouts: 6.08 us -> 3.61 us
where the time goes in v3:
time: 164 us
  Pallas kernels  160 us (98%)
  local copies, waits for them, and re-layouts  3.61 us (2%)
    pallas_call x1, Pallas kernels, shards(): pl.pallas_call(kernel, out_shape=(pltpu.VMEM(queries.shape, bf16), pltpu....  160 us
    unnamed x3, local copies, waits for them, and re-layouts  3.61 us

profile of v3, /device:TPU:1, one launch (start us, length us, event | category | flops | bytes accessed | tf_op | source)
XLA Modules:
  0.0 164.4 jit_solution(9587013259672221685)
XLA Ops:
  0.6 160.1 %shard_map.85 = (bf16[512,1024]{1,0:T(8,128)(2,1)S(1)}, bf16[8,32,16,256]{3,2,1,0:T(8,128)(2,1)S(1)}, bf16[8,32,16,256]{3,2,1,0:T(8,128)(2,1)S(1)}) custom-call(s32[6,32]{1,0:T(8,128)} %bitcast.9, bf16[512,1024]{1,0:T(8,128)(2,1)} %q_hbm.1, bf16[8,32,16,256]{3,2,1,0:T(8,128)(2,1)} %bitcast.7, bf16[8,32,16,256]{3,2,1,0:T(8,128)(2,1)} %bitcast.8, ...), custom_call_target="tpu_custom_call" | custom-call | tf_op jit(solution)/shard_map/pallas_call | solution.py:410
  160.8 1.0 copy.12
  161.7 1.3 copy.13
  163.1 1.3 copy.14

commit v4 on v3

--- a/solution.py
+++ b/solution.py
@@ -268,7 +268,7 @@
     send_in(0, 1)
     make_table()
 
-    def project(w_v):
+    def project(w_v, partial):
         w_load = pltpu.make_async_copy(w_hbm, w_v, load_sem.at[len(loads)])
         w_load.start()
         send_picks(0, 0)
@@ -279,24 +279,35 @@
         w_load.wait()
         for copy in loads:
             copy.wait()
-        wait_cotangent()
         depth = og_v.shape[2]
         half = depth // 2
+
+        def product(pair, shift, side):
+            rows = pl.ds(pair * 2 * HEAD_DIM, 2 * HEAD_DIM)
+            source = (z + shift) % ZDEV
+            part = pl.ds(pl.multiple_of(side * half, half), half)
+            columns = pl.ds(pl.multiple_of(source * depth + side * half, half), half)
+            return dot_nt(og_v[source, :, part], w_v[rows, columns])
+
         for pair in range(HEADS_HERE // 2):
-            rows = pl.ds(pair * 2 * HEAD_DIM, 2 * HEAD_DIM)
-
-            def add(t, result, rows=rows):
-                part = pl.ds(pl.multiple_of(t % 2 * half, half), half)
-                columns = pl.ds(pl.multiple_of(t * half, half), half)
-                return result + dot_nt(og_v[t // 2, :, part], w_v[rows, columns])
-
-            result = lax.fori_loop(
-                0, 2 * ZDEV, add, jnp.zeros((BLOCK, 2 * HEAD_DIM), jnp.float32)
+            partial[pair] = lax.fori_loop(
+                0,
+                2 * (ZDEV - 1),
+                lambda t, result, pair=pair: result + product(pair, t // 2 + t // 4, t % 2),
+                jnp.zeros((BLOCK, 2 * HEAD_DIM), jnp.float32),
             )
+        wait_cotangent()
+        for pair in range(HEADS_HERE // 2):
+            result = partial[pair] + product(pair, 2, 0) + product(pair, 2, 1)
             for k in range(2):
-                g_v[pair * 2 + k] = result[:, k * HEAD_DIM : (k + 1) * HEAD_DIM].astype(jnp.bfloat16)
-
-    pl.run_scoped(project, pltpu.VMEM(w_hbm.shape, jnp.bfloat16))
+                columns = slice(k * HEAD_DIM, (k + 1) * HEAD_DIM)
+                g_v[pair * 2 + k] = result[:, columns].astype(jnp.bfloat16)
+
+    pl.run_scoped(
+        project,
+        pltpu.VMEM(w_hbm.shape, jnp.bfloat16),
+        pltpu.VMEM((HEADS_HERE // 2, BLOCK, 2 * HEAD_DIM), jnp.float32),
+    )
     wait_picks(0, 0)
     wait_picks(0, 1)
 

time: 164 us -> 161 us (0.982)
  Pallas kernels: 160 us -> 157 us
    pallas_call x1, Pallas kernels: 160 us -> 157 us  [shards(): pl.pallas_call(kernel, out_shape=(pltpu.VMEM(queries.shape, bf16), pltpu....]
where the time goes in v4:
time: 161 us
  Pallas kernels  157 us (98%)
  local copies, waits for them, and re-layouts  3.61 us (2%)
    pallas_call x1, Pallas kernels, shards(): pl.pallas_call(kernel, out_shape=(pltpu.VMEM(queries.shape, bf16), pltpu....  157 us
    unnamed x3, local copies, waits for them, and re-layouts  3.61 us

profile of v4, /device:TPU:1, one launch (start us, length us, event | category | flops | bytes accessed | tf_op | source)
XLA Modules:
  0.0 161.3 jit_solution(8381256550524809686)
XLA Ops:
  0.6 157.0 %shard_map.85 = (bf16[512,1024]{1,0:T(8,128)(2,1)S(1)}, bf16[8,32,16,256]{3,2,1,0:T(8,128)(2,1)S(1)}, bf16[8,32,16,256]{3,2,1,0:T(8,128)(2,1)S(1)}) custom-call(s32[6,32]{1,0:T(8,128)} %bitcast.9, bf16[512,1024]{1,0:T(8,128)(2,1)} %q_hbm.1, bf16[8,32,16,256]{3,2,1,0:T(8,128)(2,1)} %bitcast.7, bf16[8,32,16,256]{3,2,1,0:T(8,128)(2,1)} %bitcast.8, ...), custom_call_target="tpu_custom_call" | custom-call | tf_op jit(solution)/shard_map/pallas_call | solution.py:421
  157.7 1.0 copy.12
  158.6 1.3 copy.13
  160.0 1.3 copy.14
